TPU v7x, 128 devices: a whole 4x4x4 slice. The times are simulated.
128 devices in a mesh: occ: 4 (over y), vir: 32 (over z, x, core).
Axes of the slice: x: 4, y: 4, z: 4, core: 2. Of those that a mesh axis runs over, the one named last changes fastest.
Arguments:
- amplitudes: bfloat16 [32, 32, 589824], P(None, None, ('occ', 'vir')), may hold values from -6 to 6
- ladder_integrals: bfloat16 [32, 32, 589824], P(None, None, ('occ', 'vir')), may hold values from -0.015625 to 0.015625
- driver: float32 [32, 32, 1024], P('occ', 'vir'), may hold values from -6 to 6
- occ_energy: float32 [32], replicated, may hold values from -2 to -0.5
- vir_energy: float32 [32], replicated, may hold values from 0.5 to 4
- occ_irrep: int32 [32], replicated, may hold values from 0 to 3
- vir_tile_irrep: int32 [12], replicated, may hold values from 0 to 3
Outputs:
- updated: float32 [32, 32, 1024], P('occ', 'vir')
All inputs are finite; a program needn't handle non-finite values.
Results may differ from a plain program's by a relative error of at most 0.0003.
Values sent between devices are 32-bit elements; how exact they have to be, the bound alone decides.
A program may use at most 128 MiB of HBM per device.

v0:
```python
import jax
import jax.numpy as jnp
from jax import lax
from jax.sharding import PartitionSpec as P

NV = 768
TILE = 64


def cd_labels(positions, labels):
    tiles = jnp.arange(labels.shape[0], dtype=jnp.int32)
    first = positions // NV // TILE
    second = positions % NV // TILE
    lab_first = jnp.sum(jnp.where(first[:, None] == tiles[None, :], labels[None, :], 0), axis=1)
    lab_second = jnp.sum(jnp.where(second[:, None] == tiles[None, :], labels[None, :], 0), axis=1)
    return jnp.bitwise_xor(lab_first, lab_second)


def local(amplitudes, ladder_integrals, driver, occ_energy, vir_energy, occ_irrep, vir_tile_irrep):
    occ_groups = lax.axis_size("occ")
    vir_groups = lax.axis_size("vir")
    occupied = amplitudes.shape[0]
    cd_local = amplitudes.shape[2]
    virtual = ladder_integrals.shape[0]
    occ_local = occupied // occ_groups
    vir_local = virtual // vir_groups
    rank = lax.axis_index(("occ", "vir"))
    positions = rank * cd_local + jnp.arange(cd_local, dtype=jnp.int32)
    labels = cd_labels(positions, vir_tile_irrep)
    pair_label = jnp.bitwise_xor(occ_irrep[:, None], occ_irrep[None, :])
    keep = jnp.bitwise_xor(pair_label[:, :, None], labels[None, None, :]) == 0
    masked = jnp.where(keep, amplitudes, jnp.zeros_like(amplitudes))
    product = lax.dot_general(
        masked.reshape(occupied * occupied, cd_local),
        ladder_integrals.reshape(virtual * virtual, cd_local),
        (((1,), (1,)), ((), ())),
        preferred_element_type=jnp.float32,
    )
    ladder = product.reshape(occupied, occupied, virtual, virtual)
    term = ladder.reshape(occ_groups, occ_local, occupied, vir_groups, vir_local, virtual)
    term = term.transpose(0, 3, 1, 4, 2, 5).reshape(
        occ_groups * vir_groups, occ_local, vir_local, occupied * virtual
    )
    owned = lax.psum_scatter(term, ("occ", "vir"), scatter_dimension=0, tiled=True)[0]
    own_blocks = owned.reshape(occ_local, vir_local, occupied, virtual)
    moved = lax.all_to_all(
        lax.all_to_all(own_blocks, "occ", split_axis=2, concat_axis=0, tiled=True),
        "vir",
        split_axis=3,
        concat_axis=1,
        tiled=True,
    )
    mirror = moved.transpose(2, 3, 0, 1).reshape(occ_local, vir_local, occupied * virtual)
    total = owned + mirror
    occ_rank = lax.axis_index("occ")
    vir_rank = lax.axis_index("vir")
    own_occ = lax.dynamic_slice_in_dim(occ_energy, occ_rank * occ_local, occ_local, 0)
    own_vir = lax.dynamic_slice_in_dim(vir_energy, vir_rank * vir_local, vir_local, 0)
    denom = (
        own_occ[:, None, None, None]
        + occ_energy[None, None, :, None]
        - own_vir[None, :, None, None]
        - vir_energy[None, None, None, :]
    )
    shaped = driver.reshape(occ_local, vir_local, occupied, virtual) + total.reshape(
        occ_local, vir_local, occupied, virtual
    )
    return (shaped / denom).reshape(occ_local, vir_local, occupied * virtual)


def solution(mesh):
    return jax.shard_map(
        local,
        mesh=mesh,
        in_specs=(
            P(None, None, ("occ", "vir")),
            P(None, None, ("occ", "vir")),
            P("occ", "vir", None),
            P(),
            P(),
            P(),
            P(),
        ),
        out_specs=P("occ", "vir", None),
        check_vma=False,
    )
```

profile of v0, /device:TPU:1, one launch (start us, length us, event | category | flops | bytes accessed | tf_op | source)
XLA Modules:
  0.0 768.7 jit_solution(1814649767393475776)
XLA Ops:
  6.5 0.0 reduce-scatter.2.cloned.1.call-start
  6.6 0.8 broadcast_xor_fusion
  7.4 0.9 select_reduce_fusion
  8.3 10.8 %fusion = bf16[32,32,4608]{2,1,0:T(8,128)(2,1)} fusion(bf16[32,32,4608]{2,1,0:T(8,128)(2,1)} %param.7, s32[4608]{0:T(1024)S(1)} %xor.41, s32[32,32]{1,0:T(8,128)S(1)} %broadcast_xor_fusion), kind=kLoop, calls=%fused_computation.1 | loop fusion | flops 14155776 | bytes 18896896 | tf_op jit(solution)/shard_map/jit(_where)/select_n | solution.py:32
  19.1 43.4 %fusion.3 = f32[4,32,8,1,32,32]{5,4,1,2,0,3:T(8,128)S(1)} fusion(bf16[4,8,32,4608,1]{3,2,4,1,0:T(8,128)(2,1)} %bitcast.54, bf16[32,32,4608]{2,1,0:T(8,128)(2,1)} %param.8), kind=kOutput, calls=%fused_computation.4 | convolution fusion | flops 9663676416 | bytes 23068672 | tf_op jit(solution)/shard_map/dot_general | solution.py:33
  62.5 6.2 copy.27
  68.7 13.7 %reshape.160 = f32[128,8,1,1024]{3,1,0,2:T(8,128)} reshape(f32[4,32,8,1,32,32]{5,4,2,1,0,3:T(8,128)} %copy.27) | data formatting | bytes 8388608 | tf_op jit(solution)/shard_map/reshape | solution.py:41
  82.4 0.0 reduce-scatter.2.cloned.1.call-update
  82.5 646.2 %reduce-scatter.2.cloned.1.call-done = f32[1,8,1,1024]{3,1,0,2:T(8,128)} async-done(((f32[128,8,1,1024]{3,1,0,2:T(8,128)}), f32[1,8,1,1024]{3,1,0,2:T(8,128)}) %reduce-scatter.2.cloned.1.call-update) | async-done | bytes 32784 | tf_op jit(solution)/shard_map/reduce_scatter | solution.py:44
  728.7 0.8 squeeze.3
  729.6 0.1 copy.39
  729.6 0.7 reshape.166
  730.4 3.3 all-to-all-start
  733.7 0.0 copy-done.2
  733.7 0.1 dynamic_slice.6
  733.7 0.6 dynamic_slice.7
  734.3 3.6 all-to-all-done
  737.9 0.6 broadcast.172
  738.5 0.8 reduce.1
  739.3 0.1 reshape.167
  739.4 0.1 copy.31
  739.6 0.7 reshape.168
  740.3 12.4 %all-to-all-start.1 = ((f32[32,1,256]{2,1,0:T(1,128)}), f32[32,1,256]{2,1,0:T(1,128)S(1)}, u32[]{:S(2)}, u32[]{:S(2)}) async-start(f32[32,1,256]{2,1,0:T(1,128)} %reshape.168), calls=%async_computation.2 | async-start | bytes 65536 | tf_op jit(solution)/shard_map/all_to_all | solution.py:46
  752.7 0.6 add_subtract_fusion
  753.3 0.1 reduce
  753.4 0.1 reshape.159
  753.5 6.6 all-to-all-done.1
  760.1 0.8 reduce.2
  760.8 0.1 reshape.169
  760.9 0.1 copy.32
  761.0 0.1 fusion.7
  761.2 0.7 reshape.164
  (9 shorter events, 0.1 us)
Async XLA Ops:
  6.5 722.2 %reduce-scatter.2.cloned.1.call-start = ((), (), s32[]{:S(2)}) async-start(), calls=%async_computation.3 | async-start | bytes 4227072 | tf_op jit(solution)/shard_map/reduce_scatter | solution.py:44
  68.7 665.0 %copy-start.2 = (f32[32]{0:T(128)S(1)}, f32[32]{0:T(128)}, u32[]{:S(2)}) copy-start(f32[32]{0:T(128)} %param.10) | copy-start | bytes 388
  68.7 665.0 %copy-start.1 = (f32[32]{0:T(128)S(1)}, f32[32]{0:T(128)}, u32[]{:S(2)}) copy-start(f32[32]{0:T(128)} %param.11) | copy-start | bytes 388
  68.7 684.6 %copy-start = (f32[8,1,1024]{2,1,0:T(1,128)S(1)}, f32[8,1,1024]{2,1,0:T(1,128)}, u32[]{:S(2)}) copy-start(f32[8,1,1024]{2,1,0:T(1,128)} %param.9) | copy-start | bytes 98308
  730.4 7.5 all-to-all-start
  740.3 19.8 %all-to-all-start.1 = ((f32[32,1,256]{2,1,0:T(1,128)}), f32[32,1,256]{2,1,0:T(1,128)S(1)}, u32[]{:S(2)}, u32[]{:S(2)}) async-start(f32[32,1,256]{2,1,0:T(1,128)} %reshape.168), calls=%async_computation.2 | async-start | bytes 65536 | tf_op jit(solution)/shard_map/all_to_all | solution.py:46
Sparse Core Ops, SparseCore 0:
  82.6 646.0 reduce-scatter.1
where the time goes:
time: 769 us
  waiting for transfers between devices  656 us (85%)
  matrix products  43.4 us (6%)
  local copies, waits for them, and re-layouts  24.8 us (3%)
  starting transfers between devices  15.7 us (2%)
  other arithmetic  14.9 us (2%)
  between operations  13.5 us (2%)
    reduce_scatter x1, waiting for transfers between devices, local(): lax.psum_scatter(term, ('occ', 'vir'), scatter_dimension=0, tiled=True)[0]  646 us
    dot_general x1, matrix products, local(): lax.dot_general(masked.reshape(occupied * occupied, cd_local), ladder_int...  43.4 us
  transfers between devices with their start and end apart: 3, of which 3 were waited for; matrix products, arithmetic and copies ran while one was open for 0% of the time, Pallas kernels for 0%

commit v1 on v0

v1 whole, which is shorter than its diff:
```python
import jax
import jax.numpy as jnp
from jax import lax
from jax.experimental import pallas as pl
from jax.experimental.pallas import tpu as pltpu
from jax.sharding import PartitionSpec as P

NV = 768
TILE = 64
K = 4608
KC = 1536
MESH = pl.DeviceIdType.MESH

ORDERS = ("yzx", "zxy", "xyz", "yzx", "zxy", "xyz", "zxy", "yzx")


def kernel(
    v_hbm, a_hbm, drv_hbm, occ_e, vir_e, occ_l, tile_l, out_ref,
    v, a, lab, own, oth, rc, r1, x1, r2, x2, r3, t2, ts, rm, zt, wt, drv,
    vsem, asem, dsem, csend, crecv, s1, q1, s2, q2, s3, q3, msend, mrecv,
):
    y = lax.axis_index("occ")
    w = lax.axis_index("vir")
    z, x, c = w // 8, (w // 2) % 4, w % 2
    oc = 1 - c
    me = {"y": y, "z": z, "x": x}

    def peer(axis, r):
        m = lax.rem(me[axis] + r, 4)
        if axis == "y":
            return m, (m, w)
        if axis == "z":
            return m, (y, m * 8 + x * 2 + c)
        return m, (y, z * 8 + m * 2 + c)

    partner = (y, z * 8 + x * 2 + oc)
    barrier = pltpu.get_barrier_semaphore()
    pl.semaphore_signal(barrier, inc=1, device_id=partner, device_id_type=MESH)
    for axis in "yzx":
        for r in (1, 2, 3):
            pl.semaphore_signal(barrier, inc=1, device_id=peer(axis, r)[1], device_id_type=MESH)

    def vcopy(half, core, kc):
        ks = pl.ds(kc * KC, KC)
        return pltpu.make_async_copy(v_hbm.at[:, core, :, ks], v.at[half, :, :, ks], vsem.at[half, kc])

    def acopy(p, kc):
        ks = pl.ds(kc * KC, KC)
        return pltpu.make_async_copy(a_hbm.at[:, p, :, :, ks], a.at[p, :, :, :, ks], asem.at[p, kc])

    for kc in range(3):
        vcopy(0, oc, kc).start()
        acopy(0, kc).start()
    for kc in range(3):
        vcopy(1, c, kc).start()
    for kc in range(3):
        acopy(1, kc).start()
    dcopy = pltpu.make_async_copy(drv_hbm, drv, dsem)
    dcopy.start()

    d_pos = lax.broadcasted_iota(jnp.int32, (8, NV), 1) // TILE
    d_lab = jnp.zeros((8, NV), jnp.int32)
    for t in range(NV // TILE):
        d_lab = jnp.where(d_pos == t, tile_l[t], d_lab)
    rank = y * 32 + w
    for cl in range(K // NV):
        c_lab = tile_l[(rank * (K // NV) + cl) // TILE]
        lab[:, pl.ds(cl * NV, NV)] = jnp.bitwise_xor(d_lab, c_lab)
    row = lax.broadcasted_iota(jnp.int32, (32, 128), 0)
    occ_col = jnp.zeros((32, 128), jnp.int32)
    for j in range(32):
        occ_col = jnp.where(row == j, occ_l[j], occ_col)
    occ_col = occ_col[:, :1].astype(jnp.float32).astype(jnp.bfloat16)

    def masked(p, k0, kt):
        parts = []
        base = lab[0:1, pl.ds(k0, kt)]
        for yy in range(4):
            for i in range(4):
                want = jnp.bitwise_xor(base, occ_l[yy * 8 + p * 4 + i])
                want = want.astype(jnp.float32).astype(jnp.bfloat16)
                blk = a[p, yy, i, :, pl.ds(k0, kt)]
                parts.append(jnp.where(occ_col == want, blk, jnp.zeros_like(blk)))
        return jnp.concatenate(parts, axis=0)

    def product(half, p, k0, kt):
        lhs = v[half, :, :, pl.ds(k0, kt)].reshape(512, kt)
        return lax.dot_general(
            lhs, masked(p, k0, kt), (((1,), (1,)), ((), ())), preferred_element_type=jnp.float32
        )

    def put(dst, p, d, add):
        for yy in range(4):
            blk = d[:, yy * 128:(yy + 1) * 128].reshape(4, 4, 4, 8, 128)
            if add:
                dst[p, yy] += blk
            else:
                dst[p, yy] = blk

    def core_copy(p):
        return pltpu.make_async_remote_copy(
            oth.at[p], rc.at[p], csend.at[p], crecv.at[p], device_id=partner, device_id_type=MESH
        )

    def at_axis(ref, lead, names, axis, m):
        idx = tuple(lead) + tuple(m if n == axis else slice(None) for n in names)
        return ref.at[idx]

    def stage_copies(s, p, g):
        h = p * 4 + g
        order = ORDERS[h]
        axis = order[s]
        out = []
        for r in (1, 2, 3):
            m, dev = peer(axis, r)
            if s == 0:
                src = own.at[tuple([p] + [m if n == axis else slice(None) for n in "yzx"] + [g])]
                dst, ss, rs = r1.at[h, r - 1], s1.at[h, r - 1], q1.at[h, r - 1]
            elif s == 1:
                names = [n for n in "yzx" if n != order[0]]
                src = x1.at[tuple([h] + [m if n == axis else slice(None) for n in names])]
                dst, ss, rs = r2.at[h, r - 1], s2.at[h, r - 1], q2.at[h, r - 1]
            else:
                src = x2.at[h, m]
                dst, ss, rs = r3.at[h, r - 1], s3.at[h, r - 1], q3.at[h, r - 1]
            out.append(pltpu.make_async_remote_copy(src, dst, ss, rs, device_id=dev, device_id_type=MESH))
        return out

    def stage_send(s, p, g):
        for cp in stage_copies(s, p, g):
            cp.start()

    def stage_recv(s, p, g):
        h = p * 4 + g
        order = ORDERS[h]
        axis = order[s]
        m = me[axis]
        for cp in stage_copies(s, p, g):
            cp.wait_recv()
        if s == 0:
            mine = own[tuple([p] + [m if n == axis else slice(None) for n in "yzx"] + [g])]
            x1[h] = mine + (r1[h, 0] + r1[h, 1] + r1[h, 2])
        elif s == 1:
            names = [n for n in "yzx" if n != order[0]]
            mine = x1[tuple([h] + [m if n == axis else slice(None) for n in names])]
            x2[h] = mine + (r2[h, 0] + r2[h, 1] + r2[h, 2])
        else:
            tot = x2[h, m] + (r3[h, 0] + r3[h, 1] + r3[h, 2])
            t2[p, g * 8:(g + 1) * 8, :] = tot
            ts[p, g * 8:(g + 1) * 8, 0, :] = tot

    for kc in range(3):
        vcopy(0, oc, kc).wait()
        acopy(0, kc).wait()
        put(oth, 0, product(0, 0, kc * KC, KC), kc > 0)
    pl.semaphore_wait(barrier, 10)
    core_copy(0).start()
    for kc in range(3):
        vcopy(1, c, kc).wait()
    put(own, 0, product(1, 0, 0, K), False)
    core_copy(0).wait_recv()
    own[0] = own[0] + rc[0]
    for g in range(4):
        stage_send(0, 0, g)
    for kc in range(3):
        acopy(1, kc).wait()
    put(oth, 1, product(0, 1, 0, K), False)
    core_copy(1).start()
    put(own, 1, product(1, 1, 0, K), False)
    core_copy(1).wait_recv()
    own[1] = own[1] + rc[1]
    for g in range(4):
        stage_send(0, 1, g)
    for p in range(2):
        for g in range(4):
            stage_recv(0, p, g)
            stage_send(1, p, g)
    for p in range(2):
        for g in range(4):
            stage_recv(1, p, g)
            stage_send(2, p, g)
    for p in range(2):
        for g in range(4):
            stage_recv(2, p, g)

    def send_row(r, carry):
        d = lax.rem(rank + r, 128)
        dy, dw = d // 32, lax.rem(d, 32)
        pltpu.make_async_remote_copy(
            ts.at[:, dw], rm.at[y, :, w], msend, mrecv, device_id=(dy, dw), device_id_type=MESH
        ).start()
        return carry

    pltpu.make_async_copy(ts.at[:, w], rm.at[y, :, w], mrecv).start()
    lax.fori_loop(1, 128, send_row, 0)

    lane = lax.broadcasted_iota(jnp.int32, (8, 128), 1)
    sub = lax.broadcasted_iota(jnp.int32, (8, 128), 0)
    for p in range(2):
        zt[p * 128:(p + 1) * 128, :] = jnp.concatenate([t2[p].T, jnp.zeros((128, 96), jnp.float32)], axis=1)
    dcopy.wait()
    occ_j = jnp.zeros((8, 128), jnp.float32)
    vir_b = jnp.zeros((8, 128), jnp.float32)
    jpos = sub * 4 + lane // 32
    bpos = lane % 32
    for k in range(32):
        occ_j = jnp.where(jpos == k, occ_e[k], occ_j)
        vir_b = jnp.where(bpos == k, vir_e[k], vir_b)
    mine = []
    for i in range(8):
        acc = zt[pl.ds(i * 32, 8, stride=4), :]
        for jj in range(1, 4):
            acc = acc + pltpu.roll(zt[pl.ds(i * 32 + jj, 8, stride=4), :], jj * 32, 1)
        mine.append(drv[i] + acc)

    pltpu.make_async_copy(rm, rm, mrecv).wait()
    for t in range(8):
        blk = rm[t // 2, t % 2, :, 0, :].T
        zt[0:128, :] = jnp.concatenate([blk, jnp.zeros((128, 96), jnp.float32)], axis=1)
        acc = zt[pl.ds(pl.multiple_of(y * 8, 8), 8), :]
        for jj in range(1, 4):
            acc = acc + pltpu.roll(zt[pl.ds(pl.multiple_of(jj * 32 + y * 8, 8), 8), :], jj * 32, 1)
        wt[t * 8:(t + 1) * 8, :] = acc
    va = vir_e[w]
    for i in range(8):
        tot = mine[i] + wt[pl.ds(i, 8, stride=8), :]
        den = (occ_e[y * 8 + i] + occ_j) - va - vir_b
        out_ref[i] = tot / den

    for p in range(2):
        core_copy(p).wait_send()
        for g in range(4):
            for s in range(3):
                for cp in stage_copies(s, p, g):
                    cp.wait_send()
    flat = rm.at[0:3]
    pltpu.make_async_copy(flat, flat, msend).wait()
    rest = rm.at[3, :, 0:31]
    pltpu.make_async_copy(rest, rest, msend).wait()


def local(amplitudes, ladder_integrals, driver, occ_energy, vir_energy, occ_irrep, vir_tile_irrep):
    f32, bf16 = jnp.float32, jnp.bfloat16
    dma = pltpu.SemaphoreType.DMA
    any_ = pl.BlockSpec(memory_space=pl.ANY)
    smem = pl.BlockSpec(memory_space=pltpu.SMEM)
    out = pl.pallas_call(
        kernel,
        out_shape=jax.ShapeDtypeStruct((8, 8, 128), f32),
        in_specs=[any_, any_, any_, smem, smem, smem, smem],
        out_specs=pl.BlockSpec(memory_space=pltpu.VMEM),
        scratch_shapes=[
            pltpu.VMEM((2, 16, 32, K), bf16),
            pltpu.VMEM((2, 4, 4, 32, K), bf16),
            pltpu.VMEM((8, K), jnp.int32),
            pltpu.VMEM((2, 4, 4, 4, 4, 8, 128), f32),
            pltpu.VMEM((2, 4, 4, 4, 4, 8, 128), f32),
            pltpu.VMEM((2, 4, 4, 4, 4, 8, 128), f32),
            pltpu.VMEM((8, 3, 4, 4, 8, 128), f32),
            pltpu.VMEM((8, 4, 4, 8, 128), f32),
            pltpu.VMEM((8, 3, 4, 8, 128), f32),
            pltpu.VMEM((8, 4, 8, 128), f32),
            pltpu.VMEM((8, 3, 8, 128), f32),
            pltpu.VMEM((2, 32, 128), f32),
            pltpu.VMEM((2, 32, 1, 128), f32),
            pltpu.VMEM((4, 2, 32, 1, 128), f32),
            pltpu.VMEM((256, 128), f32),
            pltpu.VMEM((64, 128), f32),
            pltpu.VMEM((8, 8, 128), f32),
            dma((2, 3)), dma((2, 3)), dma,
            dma((2,)), dma((2,)),
            dma((8, 3)), dma((8, 3)), dma((8, 3)), dma((8, 3)), dma((8, 3)), dma((8, 3)),
            dma, dma,
        ],
        compiler_params=pltpu.CompilerParams(
            collective_id=0, has_side_effects=True, vmem_limit_bytes=60 * 2**20
        ),
        name="ladder",
    )(
        ladder_integrals.reshape(16, 2, 32, K),
        amplitudes.reshape(4, 2, 4, 32, K),
        driver.reshape(8, 8, 128),
        occ_energy, vir_energy, occ_irrep, vir_tile_irrep,
    )
    return out.reshape(8, 1, 1024)


def solution(mesh):
    return jax.shard_map(
        local,
        mesh=mesh,
        in_specs=(
            P(None, None, ("occ", "vir")),
            P(None, None, ("occ", "vir")),
            P("occ", "vir", None),
            P(),
            P(),
            P(),
            P(),
        ),
        out_specs=P("occ", "vir", None),
        check_vma=False,
    )
```

time: 769 us -> 46.9 us (0.06)
  waiting for transfers between devices: 656 us -> 0 us
  Pallas kernels: 0 us -> 45.3 us
  matrix products: 43.4 us -> 0 us
  local copies, waits for them, and re-layouts: 24.8 us -> 1.38 us
  starting transfers between devices: 15.7 us -> 0 us
  other arithmetic: 14.9 us -> 0 us
  between operations: 13.5 us -> 0.01 us
    reduce_scatter x1 -> x0, waiting for transfers between devices: 646 us -> none  [local(): lax.psum_scatter(term, ('occ', 'vir'), scatter_dimension=0, tiled=True)[0]]
    pallas_call x0 -> x1, Pallas kernels: none -> 45.3 us  [local(): pl.pallas_call(kernel, out_shape=jax.ShapeDtypeStruct((8, 8, 128), f32),...]
    dot_general x1 -> x0, matrix products: 43.4 us -> none  [local(): lax.dot_general(masked.reshape(occupied * occupied, cd_local), ladder_int...]
    all_to_all x2 -> x0, starting transfers between devices: 15.7 us -> none  [the longest x1 12.4 us: local(): lax.all_to_all(lax.all_to_all(own_blocks, 'occ', split_axis=2, concat_axi...]
    reshape x3 -> x0, local copies, waits for them, and re-layouts: 14.5 us -> none  [the longest x1 13.7 us: local(): term.transpose(0, 3, 1, 4, 2, 5)]
    select_n x2 -> x0, other arithmetic: 10.9 us -> none  [the longest x1 10.8 us: local(): masked = jnp.where(keep, amplitudes, jnp.zeros_like(amplitudes))]
    all_to_all x2 -> x0, waiting for transfers between devices: 10.2 us -> none  [the longest x1 6.56 us: local(): lax.all_to_all(lax.all_to_all(own_blocks, 'occ', split_axis=2, concat_axi...]
  transfers between devices with their start and end apart: 3 -> 0, of which waited for: 3 -> 0; matrix products, arithmetic and copies ran while one was open for 0% -> 0% of each run, Pallas kernels for 0% -> 0%
where the time goes in v1:
time: 46.9 us; the launch traced here: 46.7 us
  Pallas kernels  45.3 us (97%)
  local copies, waits for them, and re-layouts  1.38 us (3%)
    pallas_call x1, Pallas kernels, local(): pl.pallas_call(kernel, out_shape=jax.ShapeDtypeStruct((8, 8, 128), f32),...  45.3 us
    unnamed x1, local copies, waits for them, and re-layouts  1.38 us

profile of v1, /device:TPU:1, one launch (start us, length us, event | category | flops | bytes accessed | tf_op | source)
XLA Modules:
  0.0 46.7 jit_solution(7673876480048351707)
XLA Ops:
  0.0 45.3 %ladder.1 = f32[8,8,128]{2,1,0:T(8,128)} custom-call(bf16[16,2,32,4608]{3,2,1,0:T(8,128)(2,1)} %bitcast.4, bf16[4,2,4,32,4608]{4,3,2,1,0:T(8,128)(2,1)} %bitcast.5, f32[8,8,128]{2,1,0:T(8,128)} %bitcast.7, f32[32]{0:T(128)} %occ_e.1, f32[32]{0:T(128)} %vir_e.1, s32[32]{0:T(128)} %occ_l.1, s32[12]{0:T(128)} %tile_l.1), custom_call_target="tpu_custom_call" | custom-call | tf_op jit(solution)/shard_map/ladder/pallas_call | solution.py:247
  45.3 1.4 %copy.10 = f32[8,1,1024]{2,1,0:T(1,128)} copy(f32[8,1,1024]{2,1,0:T(1,128)} %bitcast.6) | data formatting | bytes 65536

commit v2 on v1

--- a/solution.py
+++ b/solution.py
@@ -11,12 +11,12 @@
 KC = 1536
 MESH = pl.DeviceIdType.MESH
 
-ORDERS = ("yzx", "zxy", "xyz", "yzx", "zxy", "xyz", "zxy", "yzx")
+ORDERS = ("yzx", "zyx", "yzx", "yzx", "xzy", "zxy", "xzy", "zxy")
 
 
 def kernel(
     v_hbm, a_hbm, drv_hbm, occ_e, vir_e, occ_l, tile_l, out_ref,
-    v, a, lab, own, oth, rc, r1, x1, r2, x2, r3, t2, ts, rm, zt, wt, drv,
+    v, a, lab, own, oth, rc, r1, x1, r2, x2, r3, t2, ts, rm, et, zt, wt, drv,
     vsem, asem, dsem, csend, crecv, s1, q1, s2, q2, s3, q3, msend, mrecv,
 ):
     y = lax.axis_index("occ")
@@ -80,27 +80,33 @@
                 want = jnp.bitwise_xor(base, occ_l[yy * 8 + p * 4 + i])
                 want = want.astype(jnp.float32).astype(jnp.bfloat16)
                 blk = a[p, yy, i, :, pl.ds(k0, kt)]
-                parts.append(jnp.where(occ_col == want, blk, jnp.zeros_like(blk)))
+                blk = jnp.where(occ_col == want, blk, jnp.zeros_like(blk))
+                a[p, yy, i, :, pl.ds(k0, kt)] = blk
+                parts.append(blk)
         return jnp.concatenate(parts, axis=0)
 
-    def product(half, p, k0, kt):
-        lhs = v[half, :, :, pl.ds(k0, kt)].reshape(512, kt)
-        return lax.dot_general(
-            lhs, masked(p, k0, kt), (((1,), (1,)), ((), ())), preferred_element_type=jnp.float32
+    def unit(half, p, bh, k0, kt, dst, first, add):
+        rhs = masked(p, k0, kt) if first else a[p, :, :, :, pl.ds(k0, kt)].reshape(512, kt)
+        lhs = v[half, :, bh * 16:(bh + 1) * 16, pl.ds(k0, kt)].reshape(256, kt)
+        d = lax.dot_general(lhs, rhs, (((1,), (1,)), ((), ())), preferred_element_type=jnp.float32)
+        for yy in range(4):
+            blk = d[:, yy * 128:(yy + 1) * 128].reshape(4, 4, 2, 8, 128)
+            if add:
+                dst[p, yy, :, :, 2 * bh:2 * bh + 2] += blk
+            else:
+                dst[p, yy, :, :, 2 * bh:2 * bh + 2] = blk
+
+    def core_copy(p, bh):
+        gs = pl.ds(2 * bh, 2)
+        return pltpu.make_async_remote_copy(
+            oth.at[p, :, :, :, gs], rc.at[p, :, :, :, gs], csend.at[2 * p + bh], crecv.at[2 * p + bh],
+            device_id=partner, device_id_type=MESH,
         )
 
-    def put(dst, p, d, add):
-        for yy in range(4):
-            blk = d[:, yy * 128:(yy + 1) * 128].reshape(4, 4, 4, 8, 128)
-            if add:
-                dst[p, yy] += blk
-            else:
-                dst[p, yy] = blk
-
-    def core_copy(p):
-        return pltpu.make_async_remote_copy(
-            oth.at[p], rc.at[p], csend.at[p], crecv.at[p], device_id=partner, device_id_type=MESH
-        )
+    def core_add(p, bh):
+        core_copy(p, bh).wait_recv()
+        gs = pl.ds(2 * bh, 2)
+        own[p, :, :, :, gs] = own[p, :, :, :, gs] + rc[p, :, :, :, gs]
 
     def at_axis(ref, lead, names, axis, m):
         idx = tuple(lead) + tuple(m if n == axis else slice(None) for n in names)
@@ -147,55 +153,111 @@
         else:
             tot = x2[h, m] + (r3[h, 0] + r3[h, 1] + r3[h, 2])
             t2[p, g * 8:(g + 1) * 8, :] = tot
-            ts[p, g * 8:(g + 1) * 8, 0, :] = tot
+
+    lane = lax.broadcasted_iota(jnp.int32, (8, 128), 1)
+    sub = lax.broadcasted_iota(jnp.int32, (8, 128), 0)
+
+    def mirror_rows(p, g):
+        h = p * 4 + g
+        moved = []
+        for m in range(4):
+            val = x2[h, m]
+            out = val
+            for s in (-3, -2, -1, 1, 2, 3):
+                out = jnp.where((lane // 32) - (lane // 8) % 4 == s, pltpu.roll(val, (24 * s) % 128, 1), out)
+            moved.append(out)
+        for yy in range(4):
+            out = moved[yy]
+            for m in range(4):
+                if m != yy:
+                    out = jnp.where(lane // 32 == m, pltpu.roll(moved[m], (32 * (m - yy)) % 128, 1), out)
+            ts[p, yy, g * 8:(g + 1) * 8, 0, :] = out
+
+    red = (x, y)
+    keep = (y * 8 + z * 2 + c, w)
+
+    def mirror_send(p, bh):
+        def one(k, carry):
+            e = lax.rem(k + rank, 64)
+            dy, dw = e // 16, bh * 16 + lax.rem(e, 16)
+            src, dst = ts.at[p, dy, dw], rm.at[p, red[p], keep[p]]
+            other = dy * 32 + dw != rank
+
+            @pl.when(other)
+            def _():
+                pltpu.make_async_remote_copy(
+                    src, dst, msend.at[p], mrecv.at[p], device_id=(dy, dw), device_id_type=MESH
+                ).start()
+
+            @pl.when(jnp.logical_not(other))
+            def _():
+                pltpu.make_async_copy(src, dst, mrecv.at[p]).start()
+
+            return carry
+
+        lax.fori_loop(0, 64, one, 0)
+
+    def part(p, bh):
+        return ((p, 2 * bh), (p, 2 * bh + 1))
+
+    def first(p, bh):
+        core_add(p, bh)
+        for q in part(p, bh):
+            stage_send(0, *q)
+
+    def second(p, bh):
+        for q in part(p, bh):
+            stage_recv(0, *q)
+            stage_send(1, *q)
+
+    def third(p, bh):
+        for q in part(p, bh):
+            stage_recv(1, *q)
+            stage_send(2, *q)
+            mirror_rows(*q)
+        mirror_send(p, bh)
+
+    def last(p, bh):
+        for q in part(p, bh):
+            stage_recv(2, *q)
 
     for kc in range(3):
         vcopy(0, oc, kc).wait()
         acopy(0, kc).wait()
-        put(oth, 0, product(0, 0, kc * KC, KC), kc > 0)
+        unit(0, 0, 0, kc * KC, KC, oth, True, kc > 0)
     pl.semaphore_wait(barrier, 10)
-    core_copy(0).start()
+    core_copy(0, 0).start()
+    unit(0, 0, 1, 0, K, oth, False, False)
+    core_copy(0, 1).start()
     for kc in range(3):
         vcopy(1, c, kc).wait()
-    put(own, 0, product(1, 0, 0, K), False)
-    core_copy(0).wait_recv()
-    own[0] = own[0] + rc[0]
-    for g in range(4):
-        stage_send(0, 0, g)
+    unit(1, 0, 0, 0, K, own, False, False)
+    first(0, 0)
     for kc in range(3):
         acopy(1, kc).wait()
-    put(oth, 1, product(0, 1, 0, K), False)
-    core_copy(1).start()
-    put(own, 1, product(1, 1, 0, K), False)
-    core_copy(1).wait_recv()
-    own[1] = own[1] + rc[1]
-    for g in range(4):
-        stage_send(0, 1, g)
-    for p in range(2):
-        for g in range(4):
-            stage_recv(0, p, g)
-            stage_send(1, p, g)
-    for p in range(2):
-        for g in range(4):
-            stage_recv(1, p, g)
-            stage_send(2, p, g)
-    for p in range(2):
-        for g in range(4):
-            stage_recv(2, p, g)
-
-    def send_row(r, carry):
-        d = lax.rem(rank + r, 128)
-        dy, dw = d // 32, lax.rem(d, 32)
-        pltpu.make_async_remote_copy(
-            ts.at[:, dw], rm.at[y, :, w], msend, mrecv, device_id=(dy, dw), device_id_type=MESH
-        ).start()
-        return carry
-
-    pltpu.make_async_copy(ts.at[:, w], rm.at[y, :, w], mrecv).start()
-    lax.fori_loop(1, 128, send_row, 0)
-
-    lane = lax.broadcasted_iota(jnp.int32, (8, 128), 1)
-    sub = lax.broadcasted_iota(jnp.int32, (8, 128), 0)
+    unit(0, 1, 0, 0, K, oth, True, False)
+    core_copy(1, 0).start()
+    unit(1, 0, 1, 0, K, own, False, False)
+    first(0, 1)
+    unit(1, 1, 0, 0, K, own, False, False)
+    first(1, 0)
+    unit(0, 1, 1, 0, K, oth, False, False)
+    core_copy(1, 1).start()
+    second(0, 0)
+    unit(1, 1, 1, 0, K, own, False, False)
+    first(1, 1)
+    second(0, 1)
+    second(1, 0)
+    third(0, 0)
+    second(1, 1)
+    third(0, 1)
+    third(1, 0)
+    third(1, 1)
+    last(0, 0)
+    last(0, 1)
+    last(1, 0)
+    last(1, 1)
+
     for p in range(2):
         zt[p * 128:(p + 1) * 128, :] = jnp.concatenate([t2[p].T, jnp.zeros((128, 96), jnp.float32)], axis=1)
     dcopy.wait()
@@ -213,14 +275,22 @@
             acc = acc + pltpu.roll(zt[pl.ds(i * 32 + jj, 8, stride=4), :], jj * 32, 1)
         mine.append(drv[i] + acc)
 
-    pltpu.make_async_copy(rm, rm, mrecv).wait()
-    for t in range(8):
-        blk = rm[t // 2, t % 2, :, 0, :].T
-        zt[0:128, :] = jnp.concatenate([blk, jnp.zeros((128, 96), jnp.float32)], axis=1)
-        acc = zt[pl.ds(pl.multiple_of(y * 8, 8), 8), :]
-        for jj in range(1, 4):
-            acc = acc + pltpu.roll(zt[pl.ds(pl.multiple_of(jj * 32 + y * 8, 8), 8), :], jj * 32, 1)
-        wt[t * 8:(t + 1) * 8, :] = acc
+    for p in range(2):
+        pltpu.make_async_copy(rm.at[p], rm.at[p], mrecv.at[p]).wait()
+        for k in range(32):
+            row = (rm[p, 0, k] + rm[p, 1, k]) + (rm[p, 2, k] + rm[p, 3, k])
+            for m in range(4):
+                at = (k // 2) * 8 + m * 2 + k % 2 if p == 0 else m * 32 + k
+                et[at] = row if m == 0 else pltpu.roll(row, 128 - 32 * m, 1)
+        tr = et[:, 0, :].T
+        for yy in range(4):
+            acc = None
+            for i in range(4):
+                blk = tr[i * 8:(i + 1) * 8, :]
+                blk = blk if i == yy else pltpu.roll(blk, (32 * (i - yy)) % 128, 1)
+                acc = blk if acc is None else jnp.where(lane // 32 == i, blk, acc)
+            t = yy * 2 + p
+            wt[t * 8:(t + 1) * 8, :] = acc
     va = vir_e[w]
     for i in range(8):
         tot = mine[i] + wt[pl.ds(i, 8, stride=8), :]
@@ -228,15 +298,15 @@
         out_ref[i] = tot / den
 
     for p in range(2):
-        core_copy(p).wait_send()
+        for bh in range(2):
+            core_copy(p, bh).wait_send()
         for g in range(4):
             for s in range(3):
                 for cp in stage_copies(s, p, g):
                     cp.wait_send()
-    flat = rm.at[0:3]
-    pltpu.make_async_copy(flat, flat, msend).wait()
-    rest = rm.at[3, :, 0:31]
-    pltpu.make_async_copy(rest, rest, msend).wait()
+    for p in range(2):
+        for flat in (rm.at[p, 0:3], rm.at[p, 3, 0:31]):
+            pltpu.make_async_copy(flat, flat, msend.at[p]).wait()
 
 
 def local(amplitudes, ladder_integrals, driver, occ_energy, vir_energy, occ_irrep, vir_tile_irrep):
@@ -262,15 +332,16 @@
             pltpu.VMEM((8, 4, 8, 128), f32),
             pltpu.VMEM((8, 3, 8, 128), f32),
             pltpu.VMEM((2, 32, 128), f32),
-            pltpu.VMEM((2, 32, 1, 128), f32),
-            pltpu.VMEM((4, 2, 32, 1, 128), f32),
+            pltpu.VMEM((2, 4, 32, 1, 128), f32),
+            pltpu.VMEM((2, 4, 32, 1, 128), f32),
+            pltpu.VMEM((128, 1, 128), f32),
             pltpu.VMEM((256, 128), f32),
             pltpu.VMEM((64, 128), f32),
             pltpu.VMEM((8, 8, 128), f32),
             dma((2, 3)), dma((2, 3)), dma,
+            dma((4,)), dma((4,)),
+            dma((8, 3)), dma((8, 3)), dma((8, 3)), dma((8, 3)), dma((8, 3)), dma((8, 3)),
             dma((2,)), dma((2,)),
-            dma((8, 3)), dma((8, 3)), dma((8, 3)), dma((8, 3)), dma((8, 3)), dma((8, 3)),
-            dma, dma,
         ],
         compiler_params=pltpu.CompilerParams(
             collective_id=0, has_side_effects=True, vmem_limit_bytes=60 * 2**20

time: 46.9 us -> 43.4 us (0.925); the launches traced: 46.7 us -> 42.6 us
  Pallas kernels: 45.3 us -> 41.3 us
    pallas_call x1, Pallas kernels: 45.3 us -> 41.3 us  [local(): pl.pallas_call(kernel, out_shape=jax.ShapeDtypeStruct((8, 8, 128), f32),...]
where the time goes in v2:
time: 43.4 us; the launch traced here: 42.6 us
  Pallas kernels  41.3 us (95%)
  local copies, waits for them, and re-layouts  1.38 us (3%)
    pallas_call x1, Pallas kernels, local(): pl.pallas_call(kernel, out_shape=jax.ShapeDtypeStruct((8, 8, 128), f32),...  41.3 us
    unnamed x1, local copies, waits for them, and re-layouts  1.38 us

profile of v2, /device:TPU:1, one launch (start us, length us, event | category | flops | bytes accessed | tf_op | source)
XLA Modules:
  0.0 42.6 jit_solution(9587532871466509164)
XLA Ops:
  0.0 41.3 %ladder.1 = f32[8,8,128]{2,1,0:T(8,128)} custom-call(bf16[16,2,32,4608]{3,2,1,0:T(8,128)(2,1)} %bitcast.4, bf16[4,2,4,32,4608]{4,3,2,1,0:T(8,128)(2,1)} %bitcast.5, f32[8,8,128]{2,1,0:T(8,128)} %bitcast.7, f32[32]{0:T(128)} %occ_e.1, f32[32]{0:T(128)} %vir_e.1, s32[32]{0:T(128)} %occ_l.1, s32[12]{0:T(128)} %tile_l.1), custom_call_target="tpu_custom_call" | custom-call | tf_op jit(solution)/shard_map/ladder/pallas_call | solution.py:317
  41.3 1.4 %copy.10 = f32[8,1,1024]{2,1,0:T(1,128)} copy(f32[8,1,1024]{2,1,0:T(1,128)} %bitcast.6) | data formatting | bytes 65536

commit v3 on v2

--- a/solution.py
+++ b/solution.py
@@ -11,7 +11,7 @@
 KC = 1536
 MESH = pl.DeviceIdType.MESH
 
-ORDERS = ("yzx", "zyx", "yzx", "yzx", "xzy", "zxy", "xzy", "zxy")
+ORDERS = ("yzx", "zyx", "yzx", "yzx", "xzy", "xzy", "zxy", "xzy")
 
 
 def kernel(
@@ -86,15 +86,17 @@
         return jnp.concatenate(parts, axis=0)
 
     def unit(half, p, bh, k0, kt, dst, first, add):
+        lo, n = (0, 32) if bh is None else (bh * 16, 16)
         rhs = masked(p, k0, kt) if first else a[p, :, :, :, pl.ds(k0, kt)].reshape(512, kt)
-        lhs = v[half, :, bh * 16:(bh + 1) * 16, pl.ds(k0, kt)].reshape(256, kt)
+        lhs = v[half, :, lo:lo + n, pl.ds(k0, kt)].reshape(16 * n, kt)
         d = lax.dot_general(lhs, rhs, (((1,), (1,)), ((), ())), preferred_element_type=jnp.float32)
+        gs = slice(lo // 8, (lo + n) // 8)
         for yy in range(4):
-            blk = d[:, yy * 128:(yy + 1) * 128].reshape(4, 4, 2, 8, 128)
+            blk = d[:, yy * 128:(yy + 1) * 128].reshape(4, 4, n // 8, 8, 128)
             if add:
-                dst[p, yy, :, :, 2 * bh:2 * bh + 2] += blk
+                dst[p, yy, :, :, gs] += blk
             else:
-                dst[p, yy, :, :, 2 * bh:2 * bh + 2] = blk
+                dst[p, yy, :, :, gs] = blk
 
     def core_copy(p, bh):
         gs = pl.ds(2 * bh, 2)
@@ -224,33 +226,32 @@
     for kc in range(3):
         vcopy(0, oc, kc).wait()
         acopy(0, kc).wait()
-        unit(0, 0, 0, kc * KC, KC, oth, True, kc > 0)
+        unit(0, 0, None, kc * KC, KC, oth, True, kc > 0)
     pl.semaphore_wait(barrier, 10)
     core_copy(0, 0).start()
-    unit(0, 0, 1, 0, K, oth, False, False)
     core_copy(0, 1).start()
     for kc in range(3):
         vcopy(1, c, kc).wait()
-    unit(1, 0, 0, 0, K, own, False, False)
+        unit(1, 0, 0, kc * KC, KC, own, False, kc > 0)
     first(0, 0)
+    unit(1, 0, 1, 0, K, own, False, False)
+    first(0, 1)
     for kc in range(3):
         acopy(1, kc).wait()
     unit(0, 1, 0, 0, K, oth, True, False)
     core_copy(1, 0).start()
-    unit(1, 0, 1, 0, K, own, False, False)
-    first(0, 1)
+    unit(0, 1, 1, 0, K, oth, False, False)
+    core_copy(1, 1).start()
     unit(1, 1, 0, 0, K, own, False, False)
     first(1, 0)
-    unit(0, 1, 1, 0, K, oth, False, False)
-    core_copy(1, 1).start()
     second(0, 0)
     unit(1, 1, 1, 0, K, own, False, False)
     first(1, 1)
     second(0, 1)
+    third(0, 0)
     second(1, 0)
-    third(0, 0)
+    third(0, 1)
     second(1, 1)
-    third(0, 1)
     third(1, 0)
     third(1, 1)
     last(0, 0)

time: 43.4 us -> 42.8 us (0.986)
  Pallas kernels: 41.3 us -> 40.6 us
    pallas_call x1, Pallas kernels: 41.3 us -> 40.6 us  [local(): pl.pallas_call(kernel, out_shape=jax.ShapeDtypeStruct((8, 8, 128), f32),...]
where the time goes in v3:
time: 42.8 us; the launch traced here: 42 us
  Pallas kernels  40.6 us (95%)
  local copies, waits for them, and re-layouts  1.38 us (3%)
    pallas_call x1, Pallas kernels, local(): pl.pallas_call(kernel, out_shape=jax.ShapeDtypeStruct((8, 8, 128), f32),...  40.6 us
    unnamed x1, local copies, waits for them, and re-layouts  1.38 us

profile of v3, /device:TPU:1, one launch (start us, length us, event | category | flops | bytes accessed | tf_op | source)
XLA Modules:
  0.0 42.0 jit_solution(1079138113891429230)
XLA Ops:
  0.0 40.6 %ladder.1 = f32[8,8,128]{2,1,0:T(8,128)} custom-call(bf16[16,2,32,4608]{3,2,1,0:T(8,128)(2,1)} %bitcast.4, bf16[4,2,4,32,4608]{4,3,2,1,0:T(8,128)(2,1)} %bitcast.5, f32[8,8,128]{2,1,0:T(8,128)} %bitcast.7, f32[32]{0:T(128)} %occ_e.1, f32[32]{0:T(128)} %vir_e.1, s32[32]{0:T(128)} %occ_l.1, s32[12]{0:T(128)} %tile_l.1), custom_call_target="tpu_custom_call" | custom-call | tf_op jit(solution)/shard_map/ladder/pallas_call | solution.py:318
  40.6 1.4 %copy.10 = f32[8,1,1024]{2,1,0:T(1,128)} copy(f32[8,1,1024]{2,1,0:T(1,128)} %bitcast.6) | data formatting | bytes 65536

commit v4 on v3

--- a/solution.py
+++ b/solution.py
@@ -250,8 +250,8 @@
     second(0, 1)
     third(0, 0)
     second(1, 0)
+    second(1, 1)
     third(0, 1)
-    second(1, 1)
     third(1, 0)
     third(1, 1)
     last(0, 0)

time: 42.8 us -> 43.9 us (1.026); the launches traced: 42 us -> 43.8 us
  Pallas kernels: 40.6 us -> 42.4 us
    pallas_call x1, Pallas kernels: 40.6 us -> 42.4 us  [local(): pl.pallas_call(kernel, out_shape=jax.ShapeDtypeStruct((8, 8, 128), f32),...]
where the time goes in v4:
time: 43.9 us; the launch traced here: 43.8 us
  Pallas kernels  42.4 us (97%)
  local copies, waits for them, and re-layouts  1.38 us (3%)
    pallas_call x1, Pallas kernels, local(): pl.pallas_call(kernel, out_shape=jax.ShapeDtypeStruct((8, 8, 128), f32),...  42.4 us
    unnamed x1, local copies, waits for them, and re-layouts  1.38 us

profile of v4, /device:TPU:1, one launch (start us, length us, event | category | flops | bytes accessed | tf_op | source)
XLA Modules:
  0.0 43.8 jit_solution(6757629973501878327)
XLA Ops:
  0.0 42.4 %ladder.1 = f32[8,8,128]{2,1,0:T(8,128)} custom-call(bf16[16,2,32,4608]{3,2,1,0:T(8,128)(2,1)} %bitcast.4, bf16[4,2,4,32,4608]{4,3,2,1,0:T(8,128)(2,1)} %bitcast.5, f32[8,8,128]{2,1,0:T(8,128)} %bitcast.7, f32[32]{0:T(128)} %occ_e.1, f32[32]{0:T(128)} %vir_e.1, s32[32]{0:T(128)} %occ_l.1, s32[12]{0:T(128)} %tile_l.1), custom_call_target="tpu_custom_call" | custom-call | tf_op jit(solution)/shard_map/ladder/pallas_call | solution.py:318
  42.4 1.4 %copy.10 = f32[8,1,1024]{2,1,0:T(1,128)} copy(f32[8,1,1024]{2,1,0:T(1,128)} %bitcast.6) | data formatting | bytes 65536
